TPU v7x, 256 devices: a whole 4x4x8 slice. The times are simulated.
256 devices in a mesh: row: 16 (over y, z_lo, core), col: 16 (over x, z_hi).
Axes of the slice: x: 4, y: 4, z: 8 (z_hi: 4, z_lo: 2; z = z_hi * 2 + z_lo), core: 2. Of those that a mesh axis runs over, the one named last changes fastest.
Arguments:
- points: float32 [32, 24576], P(None, ('row', 'col')), may hold values from -6 to 6
- targets: float32 [24576], P(('row', 'col')), may hold values from -6 to 6
- probes: float32 [8, 24576], P(None, ('row', 'col')), may hold values from -6 to 6
- lengthscale: float32 [4], replicated, may hold values from 2.4 to 3.4
- outputscale: float32 [4], replicated, may hold values from 0.5 to 2
- noise_var: float32 [4], replicated, may hold values from 0.1 to 1
Outputs:
- solution: float32 [12, 24576], P(None, ('row', 'col'))
- residual: float32 [12, 24576], P(None, ('row', 'col'))
All inputs are finite; a program needn't handle non-finite values.
Results may differ from a plain program's by a relative error of at most 0.009.
Values may be sent and summed in bfloat16 or wider, within the bound.
A program may use at most 64 MiB of HBM per device.

v0:
```python
import math
import jax
import jax.numpy as jnp
from jax import lax
from jax.sharding import PartitionSpec as P

ITERATIONS = 2


def sq_distance(rows_x, cols_x):
    inner_prod = lax.dot_general(
        rows_x,
        cols_x,
        (((0,), (0,)), ((), ())),
        precision=lax.Precision.HIGHEST,
        preferred_element_type=jnp.float32,
    )
    sq_rows = jnp.sum(rows_x * rows_x, axis=0)
    sq_cols = jnp.sum(cols_x * cols_x, axis=0)
    return sq_rows[:, None] + sq_cols[None, :] - 2.0 * inner_prod


def make_tiles(distance, negscale, outputscale):
    return [
        (outputscale[p] * jnp.exp(distance * negscale[p])).astype(jnp.bfloat16)
        for p in range(negscale.shape[0])
    ]


def apply_tiles(tiles, dir_cols, width):
    products = []
    for p in range(len(tiles)):
        products.append(
            lax.dot_general(
                dir_cols[p * width : (p + 1) * width],
                tiles[p],
                (((1,), (1,)), ((), ())),
                preferred_element_type=jnp.float32,
            )
        )
    return jnp.concatenate(products, axis=0)


def on_device(points, targets, probes, lengthscale, outputscale, noise_var):
    n_part = lengthscale.shape[0]
    width = probes.shape[0] // n_part + 1
    right_side = jnp.concatenate(
        [
            jnp.concatenate(
                [targets[None, :], probes[p * (width - 1) : (p + 1) * (width - 1)]], axis=0
            )
            for p in range(n_part)
        ],
        axis=0,
    )
    negscale = -0.5 / (lengthscale * lengthscale)
    noisevec = jnp.repeat(noise_var, width)[:, None]
    rows_x = lax.all_gather(points, "col", axis=1, tiled=True)
    cols_x = lax.all_gather(points, "row", axis=1, tiled=True)
    row_count = rows_x.shape[1]
    row_block = math.gcd(row_count, 512)
    n_blocks = row_count // row_block
    kept = [
        make_tiles(
            sq_distance(rows_x[:, k * row_block : (k + 1) * row_block], cols_x),
            negscale,
            outputscale,
        )
        for k in range(n_blocks)
    ]
    solution = jnp.zeros_like(right_side)
    residual = right_side
    direction = right_side
    res_norm = lax.psum(jnp.sum(residual * residual, axis=1), ("row", "col"))
    for iteration in range(ITERATIONS):
        dir_cols = lax.all_gather(direction.astype(jnp.bfloat16), "row", axis=1, tiled=True)
        pieces = []
        for apply_k in range(n_blocks):
            tiles = kept[apply_k]
            pieces.append(apply_tiles(tiles, dir_cols, width))
        partial_value = jnp.concatenate(pieces, axis=1)
        applied = (
            lax.psum_scatter(partial_value, "col", scatter_dimension=1, tiled=True)
            + noisevec * direction
        )
        curvature = lax.psum(jnp.sum(direction * applied, axis=1), ("row", "col"))
        applied, curvature = (applied, curvature)
        step_size = (res_norm / curvature)[:, None]
        solution = solution + step_size * direction
        residual = residual - step_size * applied
        if iteration + 1 < ITERATIONS:
            fresh_norm = lax.psum(jnp.sum(residual * residual, axis=1), ("row", "col"))
            direction = residual + (fresh_norm / res_norm)[:, None] * direction
            res_norm = fresh_norm
    return (solution, residual)


def solution(mesh):
    placed = (P(None, ("row", "col")), P(("row", "col")), P(None, ("row", "col")), P(), P(), P())
    return jax.shard_map(
        on_device,
        mesh=mesh,
        in_specs=placed,
        out_specs=(P(None, ("row", "col")), P(None, ("row", "col"))),
        check_vma=False,
    )
```

profile of v0, /device:TPU:1, one launch (start us, length us, event | category | flops | bytes accessed | tf_op | source)
XLA Modules:
  0.0 570.3 jit_solution(6471585392873921023)
XLA Ops:
  7.2 22.9 %all-gather.2 = f32[16,96,32]{1,2,0:T(8,128)S(1)} all-gather(f32[1,96,32]{1,2,0:T(8,128)} %bitcast.68), channel_id=1, replica_groups=mesh['row'=16,'col'=16] {'row'}, dimensions={0}, use_global_device_ids=true | all-gather | bytes 208896 | tf_op jit(solution)/shard_map/all_gather | solution.py:59
  30.1 40.2 %all-gather.1 = f32[16,96,32]{1,2,0:T(8,128)S(1)} all-gather(f32[1,96,32]{1,2,0:T(8,128)} %bitcast.69), channel_id=1, replica_groups=mesh['row'=16,'col'=16] {'col'}, dimensions={0}, use_global_device_ids=true | all-gather | bytes 208896 | tf_op jit(solution)/shard_map/all_gather | solution.py:58
  72.7 23.2 %all-gather = bf16[16,96,12]{1,2,0:T(8,128)(2,1)S(1)} all-gather(bf16[1,96,12]{1,2,0:T(8,128)(2,1)S(1)} %convert_bitcast_fusion.1), channel_id=1, replica_groups=mesh['row'=16,'col'=16] {'row'}, dimensions={0}, use_global_device_ids=true | all-gather | bytes 39168 | tf_op jit(solution)/shard_map/all_gather | solution.py:76
  98.1 2.8 fusion
  101.0 3.7 fusion.1
  104.7 1.9 fusion.10
  106.6 1.9 fusion.18
  112.1 1.9 fusion.14
  114.0 1.9 fusion.6
  116.0 1.9 fusion.16
  117.8 1.9 fusion.8
  119.7 3.9 fusion.2
  123.6 1.8 fusion.20
  125.4 1.9 fusion.22
  127.4 1.9 fusion.24
  129.3 1.9 fusion.26
  132.7 77.2 %reduce-scatter.7.cloned.1.call-done = f32[96,12]{1,0:T(8,128)} async-done(((f32[1536,12]{1,0:T(8,128)}), f32[96,12]{1,0:T(8,128)}) %reduce-scatter.7.cloned.1.call-update) | async-done | bytes 4624
  210.9 75.8 %all-reduce = (f32[12]{0:T(128)S(1)}, f32[12]{0:T(128)S(1)}) all-reduce(f32[12]{0:T(128)S(1)} %get-tuple-element.6, f32[12]{0:T(128)S(1)} %get-tuple-element.5), channel_id=1, replica_groups=mesh['row'=16,'col'=16] {'row','col'}, use_global_device_ids=true, to_apply=%region_1.0 | all-reduce | flops 24 | bytes 192 | tf_op jit(solution)/shard_map/psum | solution.py:74
  286.9 73.4 %psum.30 = f32[12]{0:T(128)S(1)} all-reduce(f32[12]{0:T(128)S(1)} %multiply_reduce_fusion.5), channel_id=1, replica_groups=mesh['row'=16,'col'=16] {'row','col'}, use_global_device_ids=true, to_apply=%region_10.0 | all-reduce | flops 12 | bytes 96 | tf_op jit(solution)/shard_map/psum | solution.py:92
  360.4 19.8 %all-gather.3 = bf16[16,96,12]{1,2,0:T(8,128)(2,1)S(1)} all-gather(bf16[1,96,12]{1,2,0:T(8,128)(2,1)S(1)} %convert_bitcast_fusion), channel_id=1, replica_groups=mesh['row'=16,'col'=16] {'row'}, dimensions={0}, use_global_device_ids=true | all-gather | bytes 39168 | tf_op jit(solution)/shard_map/all_gather | solution.py:76
  380.4 4.0 fusion.3
  384.3 1.9 fusion.5
  386.3 1.9 fusion.7
  388.2 1.9 fusion.9
  391.9 1.9 fusion.13
  393.8 2.1 fusion.15
  396.0 1.9 fusion.17
  399.6 1.9 fusion.21
  401.6 1.9 fusion.23
  403.5 1.9 fusion.25
  406.6 79.3 %reduce-scatter.9.cloned.1.call-done = f32[96,12]{1,0:T(8,128)} async-done(((f32[1536,12]{1,0:T(8,128)}), f32[96,12]{1,0:T(8,128)}) %reduce-scatter.9.cloned.1.call-update) | async-done | bytes 4624
  487.0 75.8 %psum.31 = f32[12]{0:T(128)S(1)} all-reduce(f32[12]{0:T(128)S(1)} %multiply_reduce_fusion.4), channel_id=1, replica_groups=mesh['row'=16,'col'=16] {'row','col'}, use_global_device_ids=true, to_apply=%region_13.0 | all-reduce | flops 12 | bytes 96 | tf_op jit(solution)/shard_map/psum | solution.py:86
  (56 shorter events, 17.6 us)
Async XLA Ops:
  7.2 89.6 %copy-start.7 = (f32[4]{0:T(128)S(1)}, f32[4]{0:T(128)}, u32[]{:S(2)}) copy-start(f32[4]{0:T(128)} %param.9) | copy-start | bytes 52
  7.2 90.3 %copy-start.5 = (f32[4]{0:T(128)S(1)}, f32[4]{0:T(128)}, u32[]{:S(2)}) copy-start(f32[4]{0:T(128)} %param.10) | copy-start | bytes 52
  7.2 202.6 %reduce-scatter.7.cloned.1.call-start = ((), (), s32[]{:S(2)}) async-start(), calls=%async_computation.2 | async-start | bytes 835584
  96.7 4.3 copy-start.4
  101.0 16.9 %copy-start.2 = (f32[512,1536]{1,0:T(8,128)}, f32[512,1536]{1,0:T(8,128)S(1)}, u32[]{:S(2)}) copy-start(f32[512,1536]{1,0:T(8,128)S(1)} %fusion) | copy-start | bytes 9437188
  123.6 5.7 copy-start
  129.2 3.2 copy-start.6
  132.4 353.5 %reduce-scatter.9.cloned.1.call-start = ((), (), s32[]{:S(2)}) async-start(), calls=%async_computation.3 | async-start | bytes 835584
  380.4 4.0 copy-start.3
  393.8 4.1 copy-start.1
Sparse Core Ops, SparseCore 0:
  132.6 77.2 reduce-scatter.6
  406.8 79.0 reduce-scatter.8
where the time goes:
time: 571 us; the launch traced here: 570 us
  blocking collectives  331 us (58%)
  waiting for transfers between devices  156 us (27%)
  matrix products  58 us (10%)
  between operations  14.2 us (2%)
  local copies, waits for them, and re-layouts  8.85 us (2%)
    unnamed x4, waiting for transfers between devices  156 us
    psum x1, blocking collectives, on_device(): res_norm = lax.psum(jnp.sum(residual * residual, axis=1), ('row', 'col'))  75.8 us
    psum x1, blocking collectives, on_device(): curvature = lax.psum(jnp.sum(direction * applied, axis=1), ('row', 'col'))  75.8 us
    psum x1, blocking collectives, on_device(): fresh_norm = lax.psum(jnp.sum(residual * residual, axis=1), ('row', 'col'))  73.4 us
    dot_general x24, matrix products, apply_tiles(): lax.dot_general(dir_cols[p * width:(p + 1) * width], tiles[p], (((1,), (1...  47.6 us
    all_gather x2, blocking collectives, on_device(): lax.all_gather(direction.astype(jnp.bfloat16), 'row', axis=1, tiled=True)  43 us
    all_gather x1, blocking collectives, on_device(): rows_x = lax.all_gather(points, 'col', axis=1, tiled=True)  40.2 us
    all_gather x1, blocking collectives, on_device(): cols_x = lax.all_gather(points, 'row', axis=1, tiled=True)  22.9 us
  transfers between devices with their start and end apart: 2, of which 2 were waited for; matrix products, arithmetic and copies ran while one was open for 0% of the time, Pallas kernels for 0%

commit v1 on v0

--- a/solution.py
+++ b/solution.py
@@ -3,6 +3,7 @@
 import jax.numpy as jnp
 from jax import lax
 from jax.sharding import PartitionSpec as P
+from jax.lax import all_gather
 
 ITERATIONS = 2
 
@@ -71,7 +72,7 @@
     solution = jnp.zeros_like(right_side)
     residual = right_side
     direction = right_side
-    res_norm = lax.psum(jnp.sum(residual * residual, axis=1), ("row", "col"))
+    res_norm = jnp.sum(all_gather(jnp.sum(residual * residual, axis=1), ("row", "col")), 0)
     for iteration in range(ITERATIONS):
         dir_cols = lax.all_gather(direction.astype(jnp.bfloat16), "row", axis=1, tiled=True)
         pieces = []

time: 571 us -> 572 us (level)
    unnamed x0 -> x1, blocking collectives: none -> 76 us
    psum x1 -> x0, blocking collectives: 75.8 us -> none  [on_device(): res_norm = lax.psum(jnp.sum(residual * residual, axis=1), ('row', 'col'))]
where the time goes in v1:
time: 572 us; the launch traced here: 571 us
  blocking collectives  331 us (58%)
  waiting for transfers between devices  156 us (27%)
  matrix products  58 us (10%)
  between operations  14.2 us (2%)
  local copies, waits for them, and re-layouts  9.27 us (2%)
    unnamed x4, waiting for transfers between devices  156 us
    unnamed x1, blocking collectives  76 us
    psum x1, blocking collectives, on_device(): curvature = lax.psum(jnp.sum(direction * applied, axis=1), ('row', 'col'))  75.8 us
    psum x1, blocking collectives, on_device(): fresh_norm = lax.psum(jnp.sum(residual * residual, axis=1), ('row', 'col'))  73.5 us
    dot_general x24, matrix products, apply_tiles(): lax.dot_general(dir_cols[p * width:(p + 1) * width], tiles[p], (((1,), (1...  47.6 us
    all_gather x2, blocking collectives, on_device(): lax.all_gather(direction.astype(jnp.bfloat16), 'row', axis=1, tiled=True)  43 us
    all_gather x1, blocking collectives, on_device(): rows_x = lax.all_gather(points, 'col', axis=1, tiled=True)  40.2 us
    all_gather x1, blocking collectives, on_device(): cols_x = lax.all_gather(points, 'row', axis=1, tiled=True)  22.9 us
  transfers between devices with their start and end apart: 2, of which 2 were waited for; matrix products, arithmetic and copies ran while one was open for 0% of the time, Pallas kernels for 0%

profile of v1, /device:TPU:1, one launch (start us, length us, event | category | flops | bytes accessed | tf_op | source)
XLA Modules:
  0.0 571.0 jit_solution(7420419001252950874)
XLA Ops:
  7.2 22.9 %all-gather.3 = f32[16,96,32]{1,2,0:T(8,128)S(1)} all-gather(f32[1,96,32]{1,2,0:T(8,128)} %bitcast.68), channel_id=1, replica_groups=mesh['row'=16,'col'=16] {'row'}, dimensions={0}, use_global_device_ids=true | all-gather | bytes 208896 | tf_op jit(solution)/shard_map/all_gather | solution.py:60
  30.1 40.2 %all-gather.2 = f32[16,96,32]{1,2,0:T(8,128)S(1)} all-gather(f32[1,96,32]{1,2,0:T(8,128)} %bitcast.69), channel_id=1, replica_groups=mesh['row'=16,'col'=16] {'col'}, dimensions={0}, use_global_device_ids=true | all-gather | bytes 208896 | tf_op jit(solution)/shard_map/all_gather | solution.py:59
  72.7 23.2 %all-gather.1 = bf16[16,96,12]{1,2,0:T(8,128)(2,1)S(1)} all-gather(bf16[1,96,12]{1,2,0:T(8,128)(2,1)S(1)} %convert_bitcast_fusion.1), channel_id=1, replica_groups=mesh['row'=16,'col'=16] {'row'}, dimensions={0}, use_global_device_ids=true | all-gather | bytes 39168 | tf_op jit(solution)/shard_map/all_gather | solution.py:77
  98.1 2.8 fusion
  101.0 3.7 fusion.1
  104.7 1.9 fusion.10
  106.6 1.9 fusion.18
  112.1 1.9 fusion.14
  114.0 1.9 fusion.6
  116.0 1.9 fusion.16
  117.8 1.9 fusion.8
  119.7 3.9 fusion.2
  123.6 1.8 fusion.20
  125.4 1.9 fusion.22
  127.4 1.9 fusion.24
  129.3 1.9 fusion.26
  132.7 77.2 %reduce-scatter.7.cloned.1.call-done = f32[96,12]{1,0:T(8,128)} async-done(((f32[1536,12]{1,0:T(8,128)}), f32[96,12]{1,0:T(8,128)}) %reduce-scatter.7.cloned.1.call-update) | async-done | bytes 4624
  211.2 76.0 %all-reduce.1 = (f32[3072]{0:T(1024)S(1)}, f32[12]{0:T(128)S(1)}) all-reduce(f32[3072]{0:T(1024)S(1)} %dynamic-update-slice, f32[12]{0:T(128)S(1)} %get-tuple-element.5), channel_id=2, replica_groups=mesh['row'=16,'col'=16] {'row','col'}, use_global_device_ids=true, to_apply=%add | all-reduce | flops 3084 | bytes 24672
  287.5 73.5 %psum.22 = f32[12]{0:T(128)S(1)} all-reduce(f32[12]{0:T(128)S(1)} %multiply_reduce_fusion.5), channel_id=1, replica_groups=mesh['row'=16,'col'=16] {'row','col'}, use_global_device_ids=true, to_apply=%region_10.0 | all-reduce | flops 12 | bytes 96 | tf_op jit(solution)/shard_map/psum | solution.py:93
  361.1 19.8 %all-gather.4 = bf16[16,96,12]{1,2,0:T(8,128)(2,1)S(1)} all-gather(bf16[1,96,12]{1,2,0:T(8,128)(2,1)S(1)} %convert_bitcast_fusion), channel_id=1, replica_groups=mesh['row'=16,'col'=16] {'row'}, dimensions={0}, use_global_device_ids=true | all-gather | bytes 39168 | tf_op jit(solution)/shard_map/all_gather | solution.py:77
  381.1 4.0 fusion.3
  385.0 1.9 fusion.5
  387.0 1.9 fusion.7
  388.9 1.9 fusion.9
  392.6 1.9 fusion.13
  394.5 2.1 fusion.15
  396.6 1.9 fusion.17
  400.3 1.9 fusion.21
  402.3 1.9 fusion.23
  404.2 1.9 fusion.25
  407.3 79.3 %reduce-scatter.9.cloned.1.call-done = f32[96,12]{1,0:T(8,128)} async-done(((f32[1536,12]{1,0:T(8,128)}), f32[96,12]{1,0:T(8,128)}) %reduce-scatter.9.cloned.1.call-update) | async-done | bytes 4624
  487.6 75.8 %psum.23 = f32[12]{0:T(128)S(1)} all-reduce(f32[12]{0:T(128)S(1)} %multiply_reduce_fusion.4), channel_id=1, replica_groups=mesh['row'=16,'col'=16] {'row','col'}, use_global_device_ids=true, to_apply=%region_13.0 | all-reduce | flops 12 | bytes 96 | tf_op jit(solution)/shard_map/psum | solution.py:87
  (60 shorter events, 18.0 us)
Async XLA Ops:
  7.2 89.6 %copy-start.7 = (f32[4]{0:T(128)S(1)}, f32[4]{0:T(128)}, u32[]{:S(2)}) copy-start(f32[4]{0:T(128)} %param.9) | copy-start | bytes 52
  7.2 90.3 %copy-start.5 = (f32[4]{0:T(128)S(1)}, f32[4]{0:T(128)}, u32[]{:S(2)}) copy-start(f32[4]{0:T(128)} %param.10) | copy-start | bytes 52
  7.2 202.6 %reduce-scatter.7.cloned.1.call-start = ((), (), s32[]{:S(2)}) async-start(), calls=%async_computation.2 | async-start | bytes 835584
  96.7 4.3 copy-start.4
  101.0 16.9 %copy-start.2 = (f32[512,1536]{1,0:T(8,128)}, f32[512,1536]{1,0:T(8,128)S(1)}, u32[]{:S(2)}) copy-start(f32[512,1536]{1,0:T(8,128)S(1)} %fusion) | copy-start | bytes 9437188
  123.6 5.7 copy-start
  129.2 3.2 copy-start.6
  132.4 354.1 %reduce-scatter.9.cloned.1.call-start = ((), (), s32[]{:S(2)}) async-start(), calls=%async_computation.3 | async-start | bytes 835584
  381.0 4.0 copy-start.3
  394.5 4.1 copy-start.1
Sparse Core Ops, SparseCore 0:
  132.6 77.2 reduce-scatter.6
  407.5 79.0 reduce-scatter.8
